TPU v7x, 32 devices: a whole 2x2x4 slice. The times are simulated.
32 devices in a mesh: groups: 2 (over x), gx: 16 (over z, y, core).
Axes of the slice: x: 2, y: 2, z: 4, core: 2. Of those that a mesh axis runs over, the one named last changes fastest.
Arguments:
- snapshots: bfloat16 [256, 4, 512, 128], P('gx', None, 'groups'), parts along dimension 2, may hold values from -20 to 20
- cell_weights: float32 [512, 128], P(('groups', 'gx')), parts along dimension 0, may hold values from 0.5 to 4.5
- diffusivity: float32 [4, 512, 128], P(None, ('groups', 'gx')), parts along dimension 1, may hold values from 0.2 to 2
Outputs:
- diffused_modes: bfloat16 [256, 4, 512, 128], P(None, None, ('groups', 'gx')), parts along dimension 2
- reduced_operator: float32 [512, 256], P('groups'), parts along dimension 0
There are 2 independent parts, one for each index of `groups`. A program takes and returns all parts, laid end to end along the dimension named above; each array names one. Nothing has to cross between parts.
All inputs are finite; a program needn't handle non-finite values.
Results may differ from a plain program's by a relative error of at most 0.0005.
Values may be sent and summed in bfloat16 or wider, within the bound.
A program may use at most 128 MiB of HBM per device.

v0:
```python
import jax
import jax.numpy as jnp
from jax import lax
from jax.sharding import PartitionSpec as P


def extended(block, sides, width):
    for axis, dim in sides:
        count = lax.axis_size(axis)
        forward = [(i, i + 1) for i in range(count - 1)]
        backward = [(target, source) for source, target in forward]
        low = lax.ppermute(
            lax.slice_in_dim(block, block.shape[dim] - width, None, axis=dim), axis, forward
        )
        high = lax.ppermute(lax.slice_in_dim(block, 0, width, axis=dim), axis, backward)
        block = jnp.concatenate([low, block, high], axis=dim)
    return block


def stencil_apply(padded_x, diffusivity):
    field = padded_x[:, :, 2:-2]
    along_x = (
        -padded_x[:, :, :-4]
        + 16.0 * padded_x[:, :, 1:-3]
        - 30.0 * field
        + 16.0 * padded_x[:, :, 3:-1]
        - padded_x[:, :, 4:]
    ) / 12.0
    padded_y = jnp.pad(field, ((0, 0), (0, 0), (0, 0), (2, 2)))
    along_y = (
        -padded_y[..., :-4]
        + 16.0 * padded_y[..., 1:-3]
        - 30.0 * field
        + 16.0 * padded_y[..., 3:-1]
        - padded_y[..., 4:]
    ) / 12.0
    return diffusivity * (along_x + along_y)


def make_rotation(gram_total):
    lower_factor = jnp.linalg.cholesky(gram_total)
    identity = jnp.eye(gram_total.shape[0], dtype=jnp.float32)
    return jax.scipy.linalg.solve_triangular(lower_factor, identity, lower=True)


def on_device(snapshots, cell_weights, diffusivity):
    highest = lax.Precision.HIGHEST
    pod_block = lax.all_to_all(snapshots, "gx", split_axis=2, concat_axis=0, tiled=True)
    snap_float = pod_block.astype(jnp.float32)
    gram_part = jnp.einsum(
        "svxy,tvxy->st", snap_float, snap_float * cell_weights, precision=highest
    )
    cell_count = pod_block.shape[1] * pod_block.shape[2] * pod_block.shape[3] * lax.axis_size("gx")
    padded_raw = extended(pod_block, (("gx", 2),), 2)
    diffused_raw = stencil_apply(padded_raw.astype(jnp.float32), diffusivity)
    cross_part = jnp.einsum(
        "svxy,tvxy->st", snap_float * cell_weights, diffused_raw, precision=highest
    )
    gram_sum_all, cross_sum_all = lax.psum((gram_part, cross_part), "gx")
    rotation = make_rotation(gram_sum_all / cell_count)
    cross_total = cross_sum_all / cell_count
    reduced = jnp.dot(
        jnp.dot(rotation, cross_total, precision=highest), rotation.T, precision=highest
    )
    diffused = jnp.einsum("st,tvxy->svxy", rotation, diffused_raw, precision=highest)
    return (diffused.astype(jnp.bfloat16), reduced)


def solution(mesh):
    in_specs = (
        P("gx", None, "groups", None),
        P(("groups", "gx"), None),
        P(None, ("groups", "gx"), None),
    )
    out_specs = (P(None, None, ("groups", "gx"), None), P("groups", None))
    return jax.shard_map(
        on_device, mesh=mesh, in_specs=in_specs, out_specs=out_specs, check_vma=False
    )
```

profile of v0, /device:TPU:0, one launch (start us, length us, event | category | flops | bytes accessed | tf_op | source)
XLA Modules:
  0.0 352.7 jit_solution(6415887800945460660)
XLA Ops:
  7.2 0.0 copy-start.3
  7.2 6.9 %copy.12 = bf16[16,4,256,128]{3,0,1,2:T(8,128)(2,1)} copy(bf16[16,4,256,128]{3,2,1,0:T(8,128)(2,1)} %param.3) | data formatting | bytes 8388608 | tf_op args[0]
  14.1 7.6 %all-to-all-start = ((bf16[16,4,256,128]{3,0,1,2:T(8,128)(2,1)}), bf16[16,4,256,128]{3,0,1,2:T(8,128)(2,1)}, u32[]{:S(2)}, u32[]{:S(2)}) async-start(bf16[16,4,256,128]{3,0,1,2:T(8,128)(2,1)} %copy.12), calls=%async_computation | async-start | bytes 8388608 | tf_op jit(solution)/shard_map/all_to_all | solution.py:48
  21.7 0.0 all-reduce.5.cloned.1.call-start
  21.7 0.0 copy-done.3
  21.8 77.5 %all-to-all-done = bf16[16,4,256,128]{3,0,1,2:T(8,128)(2,1)} async-done(((bf16[16,4,256,128]{3,0,1,2:T(8,128)(2,1)}), bf16[16,4,256,128]{3,0,1,2:T(8,128)(2,1)}, u32[]{:S(2)}, u32[]{:S(2)}) %all-to-all-start) | async-done | bytes 4194336 | tf_op jit(solution)/shard_map/all_to_all | solution.py:48
  99.2 3.4 copy.13
  102.6 0.0 copy-start
  102.6 0.1 fusion.37
  102.7 2.9 collective-permute-start
  105.7 1.8 collective-permute-start.1
  107.4 0.0 copy-done.2
  107.4 3.3 convert_multiply_fusion
  110.7 4.5 %convolution_bitcast_fusion = f32[256,256]{0,1:T(8,128)} fusion(f32[256,4,16,128]{3,0,2,1:T(8,128)S(1)} %bitcast.59, bf16[256,4,16,128]{3,0,2,1:T(8,128)(2,1)S(1)} %bitcast.56), kind=kOutput, calls=%fused_computation.30 | convolution fusion | flops 6442450944 | bytes 12845056 | tf_op jit(solution)/shard_map/svxy,tvxy->st/dot_general | solution.py:50
  115.2 0.0 copy-done
  115.2 0.0 collective-permute-done
  115.2 0.0 collective-permute-done.1
  115.2 2.7 maximum_convert_fusion
  117.9 3.8 %slice.107 = f32[256,4,16,128]{3,0,2,1:T(8,128)} slice(f32[256,4,20,128]{3,0,2,1:T(8,128)S(1)} %maximum_convert_fusion), slice={[0:256], [0:4], [2:18], [0:128]} | slice | bytes 16777216 | tf_op jit(solution)/shard_map/slice | solution.py:21
  121.7 24.1 %fusion.6 = f32[256,4,16,128]{3,0,2,1:T(8,128)} fusion(f32[256,4,16,128]{3,0,2,1:T(8,128)} %slice.107, f32[256,4,20,128]{3,0,2,1:T(8,128)S(1)} %maximum_convert_fusion, f32[4,16,128]{2,1,0:T(8,128)S(1)} %broadcast_multiply_fusion.1), kind=kLoop, calls=%fused_computation.12 | loop fusion | flops 35651584 | bytes 50364416 | tf_op jit(solution)/shard_map/mul | solution.py:37
  145.8 11.2 %fusion.16 = f32[256,256]{0,1:T(8,128)} fusion(f32[256,4,16,128]{3,0,2,1:T(8,128)} %fusion.6, bf16[256,4,16,128]{3,0,2,1:T(8,128)(2,1)} %bitcast.58, f32[16,128]{1,0:T(8,128)S(1)} %copy-done.2), kind=kOutput, calls=%fused_computation.29 | convolution fusion | flops 6446645248 | bytes 12853248 | tf_op jit(solution)/shard_map/svxy,tvxy->st/dot_general | solution.py:56
  157.0 0.0 all-reduce.5.cloned.1.call-update
  157.1 109.4 %all-reduce.5.cloned.1.call-done = (f32[256,256]{0,1:T(8,128)}, f32[256,256]{0,1:T(8,128)}) async-done(((f32[256,256]{0,1:T(8,128)}, f32[256,256]{0,1:T(8,128)}), (f32[256,256]{0,1:T(8,128)}, f32[256,256]{0,1:T(8,128)})) %all-reduce.5.cloned.1.call-update) | async-done | bytes 524304 | tf_op jit(solution)/shard_map/psum | solution.py:59
  266.5 1.0 broadcast_multiply_fusion
  267.5 0.1 copy.14
  267.6 1.0 fusion.20
  268.6 11.7 %cholesky.50 = f32[128,128]{1,0:T(8,128)S(1)} custom-call(f32[128,128]{1,0:T(8,128)S(1)} %cholesky.118), custom_call_target="Cholesky" | custom-call | tf_op jit(solution)/shard_map/jit(cholesky)/cholesky | solution.py:41
  280.3 9.8 %custom-call.15 = f32[1,128,128]{1,2,0:T(8,128)S(1)} custom-call(f32[1,128,128]{2,1,0:T(8,128)S(1)} %get-tuple-element.33), custom_call_target="InvertDiagBlocksLowerTriangular" | custom-call | tf_op jit(solution)/shard_map/jit(cholesky)/cholesky | solution.py:41
  290.2 0.2 constant_dynamic-update-slice_fusion.1
  290.4 0.3 convolution_subtract_fusion.1
  290.7 11.7 %cholesky.105 = f32[128,128]{1,0:T(8,128)S(1)} custom-call(f32[128,128]{1,0:T(8,128)S(1)} %convolution_subtract_fusion.1), custom_call_target="Cholesky" | custom-call | tf_op jit(solution)/shard_map/jit(cholesky)/cholesky | solution.py:41
  302.4 0.7 compare_reduce_fusion
  304.5 0.1 triangular_solve.63
  304.6 4.1 %while.1 = (s32[]{:T(128)}, f32[256,256]{1,0:T(8,128)S(1)}, s32[2,2]{1,0:T(2,128)S(1)}, f32[2,128,128]{2,1,0:T(8,128)S(1)}, s32[]{:T(128)}) while((s32[]{:T(128)}, f32[256,256]{1,0:T(8,128)S(1)}, s32[2,2]{1,0:T(2,128)S(1)}, f32[2,128,128]{2,1,0:T(8,128)S(1)}, s32[]{:T(128)}) %tuple.31), condition=%wide.while_cond, body=%wide.while_body.sunk | while | flops 2 | bytes 131189 | solution.py:43
  304.6 0.6 fusion.48
  305.2 1.4 bitcast_dynamic-update-slice_fusion.2
  306.6 0.6 fusion.48
  307.2 1.4 bitcast_dynamic-update-slice_fusion.2
  308.6 19.9 %custom-call.16 = f32[2,128,128]{1,2,0:T(8,128)S(1)} custom-call(f32[2,128,128]{2,1,0:T(8,128)S(1)} %get-tuple-element.9), custom_call_target="InvertDiagBlocksLowerTriangular" | custom-call | tf_op jit(solution)/shard_map/jit(_solve_triangular)/triangular_solve | solution.py:43
  328.5 0.3 fusion.25
  328.8 0.3 convolution_subtract_fusion
  329.1 0.3 fusion.28
  329.4 0.0 copy-start.1
  329.4 10.0 %convolution_convert_fusion = bf16[256,4,16,128]{3,0,2,1:T(8,128)(2,1)S(1)} fusion(f32[256,4,16,128]{3,0,2,1:T(8,128)} %fusion.6, f32[128,256]{1,0:T(8,128)S(1)} %fusion.28, f32[128,256]{1,0:T(8,128)S(1)} %fusion.25), kind=kOutput, calls=%fused_computation.28 | convolution fusion | flops 6444613632 | bytes 12845056 | tf_op jit(solution)/shard_map/st,tvxy->svxy/dot_general | solution.py:65
  339.4 4.7 %copy.16 = bf16[256,4,16,128]{3,2,1,0:T(8,128)(2,1)} copy(bf16[256,4,16,128]{3,0,2,1:T(8,128)(2,1)S(1)} %convolution_convert_fusion) | data formatting | bytes 8388608
  344.1 0.0 copy-done.1
  344.1 0.4 fusion.21
  344.6 1.1 fusion.23
  (12 shorter events, 0.2 us)
Async XLA Ops:
  7.2 14.6 %copy-start.3 = (f32[4,16,128]{2,1,0:T(8,128)S(1)}, f32[4,16,128]{2,1,0:T(8,128)}, u32[]{:S(2)}) copy-start(f32[4,16,128]{2,1,0:T(8,128)} %param.5) | copy-start | bytes 98308
  14.1 93.3 %copy-start.2 = (f32[16,128]{1,0:T(8,128)S(1)}, f32[16,128]{1,0:T(8,128)}, u32[]{:S(2)}) copy-start(f32[16,128]{1,0:T(8,128)} %param.4) | copy-start | bytes 24580
  14.1 85.1 %all-to-all-start = ((bf16[16,4,256,128]{3,0,1,2:T(8,128)(2,1)}), bf16[16,4,256,128]{3,0,1,2:T(8,128)(2,1)}, u32[]{:S(2)}, u32[]{:S(2)}) async-start(bf16[16,4,256,128]{3,0,1,2:T(8,128)(2,1)} %copy.12), calls=%async_computation | async-start | bytes 8388608 | tf_op jit(solution)/shard_map/all_to_all | solution.py:48
  21.7 244.8 %all-reduce.5.cloned.1.call-start = ((), (), s32[]{:S(2)}) async-start(), calls=%async_computation.1 | async-start | bytes 1048576 | tf_op jit(solution)/shard_map/psum | solution.py:59
  102.6 12.6 %copy-start = (bf16[16,4,16,16,128]{4,0,2,3,1:T(8,128)(2,1)}, bf16[16,4,16,16,128]{4,0,2,3,1:T(8,128)(2,1)S(1)}, u32[]{:S(2)}) copy-start(bf16[16,4,16,16,128]{4,0,2,3,1:T(8,128)(2,1)S(1)} %copy.13) | copy-start | bytes 12582916
  102.7 12.5 %collective-permute-start = (bf16[256,4,2,128]{3,0,2,1:T(8,128)(2,1)S(1)}, bf16[256,4,2,128]{3,0,2,1:T(8,128)(2,1)S(1)}, u32[]{:S(2)}, u32[]{:S(2)}) collective-permute-start(bf16[256,4,2,128]{3,0,2,1:T(8,128)(2,1)S(1)} %get-tuple-element.28), channel_id=1, source_target_pairs={{0,1},{1,2},{2,3},{3,4},{4,5},{5,6},{6,7},{7,8},{8,9},{9,10},{10,1... | collective-permute-start | bytes 1572872 | tf_op jit(solution)/shard_map/ppermute | solution.py:12
  105.7 9.6 %collective-permute-start.1 = (bf16[256,4,2,128]{3,0,2,1:T(8,128)(2,1)S(1)}, bf16[256,4,2,128]{3,0,2,1:T(8,128)(2,1)S(1)}, u32[]{:S(2)}, u32[]{:S(2)}) collective-permute-start(bf16[256,4,2,128]{3,0,2,1:T(8,128)(2,1)S(1)} %get-tuple-element.29), channel_id=1, source_target_pairs={{1,0},{2,1},{3,2},{4,3},{5,4},{6,5},{7,6},{8,7},{9,8},{10,9},{11,1... | collective-permute-start | bytes 1572872 | tf_op jit(solution)/shard_map/ppermute | solution.py:15
  329.4 14.8 %copy-start.1 = (f32[256,256]{0,1:T(8,128)S(1)}, f32[256,256]{0,1:T(8,128)}, u32[]{:S(2)}) copy-start(f32[256,256]{0,1:T(8,128)} %get-tuple-element.25) | copy-start | bytes 786436
Sparse Core Ops, SparseCore 0:
  157.1 109.2 all-reduce.4
where the time goes:
time: 357 us; the launch traced here: 353 us
  waiting for transfers between devices  187 us (52%)
  other arithmetic  86 us (24%)
  matrix products  28.6 us (8%)
  local copies, waits for them, and re-layouts  23.1 us (6%)
  between operations  15.8 us (4%)
  starting transfers between devices  12.3 us (3%)
    psum x1, waiting for transfers between devices, on_device(): gram_sum_all, cross_sum_all = lax.psum((gram_part, cross_part), 'gx')  109 us
    all_to_all x1, waiting for transfers between devices, on_device(): lax.all_to_all(snapshots, 'gx', split_axis=2, concat_axis=0, tiled=True)  77.5 us
    another operation x6, other arithmetic, make_rotation(): lower_factor = jnp.linalg.cholesky(gram_total)  34 us
    mul x2, other arithmetic, stencil_apply(): return diffusivity * (along_x + along_y)  24.1 us
    another operation x3, other arithmetic, make_rotation(): return jax.scipy.linalg.solve_triangular(lower_factor, identity, lower=True)  19.9 us
    unnamed x10, local copies, waits for them, and re-layouts  11.6 us
    dot_general x1, matrix products, on_device(): jnp.einsum('svxy,tvxy->st', snap_float * cell_weights, diffused_raw, prec...  11.2 us
    dot_general x1, matrix products, on_device(): jnp.einsum('st,tvxy->svxy', rotation, diffused_raw, precision=highest)  10 us
  transfers between devices with their start and end apart: 4, of which 2 were waited for; matrix products, arithmetic and copies ran while one was open for 2% of the time, Pallas kernels for 0%

commit v1 on v0

--- a/solution.py
+++ b/solution.py
@@ -45,7 +45,15 @@
 
 def on_device(snapshots, cell_weights, diffusivity):
     highest = lax.Precision.HIGHEST
-    pod_block = lax.all_to_all(snapshots, "gx", split_axis=2, concat_axis=0, tiled=True)
+    pod_block = jnp.concatenate(
+        lax.all_to_all(
+            jnp.stack(jnp.split(snapshots, lax.axis_size("gx"), 2)),
+            "gx",
+            split_axis=0,
+            concat_axis=0,
+        ),
+        0,
+    )
     snap_float = pod_block.astype(jnp.float32)
     gram_part = jnp.einsum(
         "svxy,tvxy->st", snap_float, snap_float * cell_weights, precision=highest

time: 357 us -> 382 us (1.070)
  local copies, waits for them, and re-layouts: 23.1 us -> 44.6 us
  matrix products: 28.6 us -> 33.6 us
    unnamed x10 -> x24, local copies, waits for them, and re-layouts: 11.6 us -> 29.9 us
    dot_general x1, matrix products: 4.48 us -> 9.58 us  [on_device(): jnp.einsum('svxy,tvxy->st', snap_float, snap_float * cell_weights, precis...]
  transfers between devices with their start and end apart: 4 -> 4, of which waited for: 2 -> 2; matrix products, arithmetic and copies ran while one was open for 2% -> 3% of each run, Pallas kernels for 0% -> 0%
where the time goes in v1:
time: 382 us; the launch traced here: 378 us
  waiting for transfers between devices  185 us (48%)
  other arithmetic  86.6 us (23%)
  local copies, waits for them, and re-layouts  44.6 us (12%)
  matrix products  33.6 us (9%)
  between operations  15.8 us (4%)
  starting transfers between devices  12.1 us (3%)
    psum x1, waiting for transfers between devices, on_device(): gram_sum_all, cross_sum_all = lax.psum((gram_part, cross_part), 'gx')  108 us
    all_to_all x1, waiting for transfers between devices, on_device(): lax.all_to_all(jnp.stack(jnp.split(snapshots, lax.axis_size('gx'), 2)), '...  77.5 us
    another operation x6, other arithmetic, make_rotation(): lower_factor = jnp.linalg.cholesky(gram_total)  34 us
    unnamed x24, local copies, waits for them, and re-layouts  29.9 us
    mul x2, other arithmetic, stencil_apply(): return diffusivity * (along_x + along_y)  24.1 us
    another operation x3, other arithmetic, make_rotation(): return jax.scipy.linalg.solve_triangular(lower_factor, identity, lower=True)  19.9 us
    dot_general x1, matrix products, on_device(): jnp.einsum('svxy,tvxy->st', snap_float * cell_weights, diffused_raw, prec...  11.2 us
    dot_general x1, matrix products, on_device(): jnp.einsum('st,tvxy->svxy', rotation, diffused_raw, precision=highest)  9.98 us
  transfers between devices with their start and end apart: 4, of which 2 were waited for; matrix products, arithmetic and copies ran while one was open for 3% of the time, Pallas kernels for 0%

profile of v1, /device:TPU:0, one launch (start us, length us, event | category | flops | bytes accessed | tf_op | source)
XLA Modules:
  0.0 378.0 jit_solution(3568269106964519062)
XLA Ops:
  7.2 1.7 bitcast_dynamic-update-slice_fusion.16
  8.8 1.7 bitcast_dynamic-update-slice_fusion.15
  10.5 1.7 bitcast_dynamic-update-slice_fusion.14
  12.2 1.7 bitcast_dynamic-update-slice_fusion.13
  13.9 1.7 bitcast_dynamic-update-slice_fusion.12
  15.6 1.7 bitcast_dynamic-update-slice_fusion.11
  17.2 1.7 bitcast_dynamic-update-slice_fusion.10
  18.9 1.7 bitcast_dynamic-update-slice_fusion.9
  20.6 1.7 bitcast_dynamic-update-slice_fusion.8
  22.3 1.7 bitcast_dynamic-update-slice_fusion.7
  24.0 1.7 bitcast_dynamic-update-slice_fusion.6
  25.6 1.7 bitcast_dynamic-update-slice_fusion.5
  27.3 1.7 bitcast_dynamic-update-slice_fusion.4
  29.0 1.7 bitcast_dynamic-update-slice_fusion.3
  30.7 1.7 bitcast_dynamic-update-slice_fusion.2
  32.4 1.7 bitcast_dynamic-update-slice_fusion.1
  34.0 7.6 %all-to-all-start = ((bf16[16,16,4,16,128]{4,3,2,1,0:T(8,128)(2,1)}), bf16[16,16,4,16,128]{4,3,2,1,0:T(8,128)(2,1)}, u32[]{:S(2)}, u32[]{:S(2)}) async-start(bf16[16,16,4,16,128]{4,3,2,1,0:T(8,128)(2,1)} %bitcast_dynamic-update-slice_fusion.1), calls=%async_computation | async-start | bytes 8388608 | tf_op jit(solution)/shard_map/all_to_all | solution.py:49
  41.7 77.5 %all-to-all-done = bf16[16,16,4,16,128]{4,3,2,1,0:T(8,128)(2,1)} async-done(((bf16[16,16,4,16,128]{4,3,2,1,0:T(8,128)(2,1)}), bf16[16,16,4,16,128]{4,3,2,1,0:T(8,128)(2,1)}, u32[]{:S(2)}, u32[]{:S(2)}) %all-to-all-start) | async-done | bytes 4194336 | tf_op jit(solution)/shard_map/all_to_all | solution.py:49
  119.2 4.9 %copy.5 = bf16[16,16,4,16,128]{4,1,0,3,2:T(8,128)(2,1)S(1)} copy(bf16[16,16,4,16,128]{4,3,2,1,0:T(8,128)(2,1)} %all-to-all-done) | data formatting | bytes 8388608 | tf_op jit(solution)/shard_map/all_to_all | solution.py:49
  124.2 2.9 collective-permute-start
  127.1 1.6 collective-permute-start.1
  128.7 3.4 convert_multiply_fusion
  132.1 9.6 %fusion.21 = f32[256,256]{0,1:T(8,128)} fusion(bf16[256,4,16,128]{3,0,2,1:T(8,128)(2,1)S(1)} %bitcast.81, f32[256,4,16,128]{3,2,1,0:T(8,128)S(1)} %bitcast.84), kind=kOutput, calls=%fused_computation.32 | convolution fusion | flops 6442450944 | bytes 12845056 | tf_op jit(solution)/shard_map/svxy,tvxy->st/dot_general | solution.py:58
  141.7 3.2 maximum_convert_fusion
  144.9 3.8 slice.107
  148.6 24.1 %fusion.6 = f32[256,4,16,128]{3,0,2,1:T(8,128)} fusion(f32[256,4,16,128]{3,0,2,1:T(8,128)} %slice.107, f32[256,4,20,128]{3,0,2,1:T(8,128)S(1)} %maximum_convert_fusion, f32[4,16,128]{2,1,0:T(8,128)S(1)} %broadcast_multiply_fusion.1), kind=kLoop, calls=%fused_computation.12 | loop fusion | flops 35651584 | bytes 50364416 | tf_op jit(solution)/shard_map/mul | solution.py:37
  172.7 11.2 %fusion.18 = f32[256,256]{0,1:T(8,128)} fusion(f32[256,4,16,128]{3,0,2,1:T(8,128)} %fusion.6, bf16[256,4,16,128]{3,0,2,1:T(8,128)(2,1)} %bitcast.83, f32[16,128]{1,0:T(8,128)S(1)} %copy-done.2), kind=kOutput, calls=%fused_computation.31 | convolution fusion | flops 6446645248 | bytes 12853248 | tf_op jit(solution)/shard_map/svxy,tvxy->st/dot_general | solution.py:64
  184.1 107.7 %all-reduce.5.cloned.1.call-done = (f32[256,256]{0,1:T(8,128)}, f32[256,256]{0,1:T(8,128)}) async-done(((f32[256,256]{0,1:T(8,128)}, f32[256,256]{0,1:T(8,128)}), (f32[256,256]{0,1:T(8,128)}, f32[256,256]{0,1:T(8,128)})) %all-reduce.5.cloned.1.call-update) | async-done | bytes 524304 | tf_op jit(solution)/shard_map/psum | solution.py:67
  291.7 1.0 broadcast_multiply_fusion
  292.8 1.0 fusion.25
  293.8 11.7 %cholesky.50 = f32[128,128]{1,0:T(8,128)S(1)} custom-call(f32[128,128]{1,0:T(8,128)S(1)} %cholesky.118), custom_call_target="Cholesky" | custom-call | tf_op jit(solution)/shard_map/jit(cholesky)/cholesky | solution.py:41
  305.6 9.8 %custom-call.15 = f32[1,128,128]{1,2,0:T(8,128)S(1)} custom-call(f32[1,128,128]{2,1,0:T(8,128)S(1)} %get-tuple-element.29), custom_call_target="InvertDiagBlocksLowerTriangular" | custom-call | tf_op jit(solution)/shard_map/jit(cholesky)/cholesky | solution.py:41
  315.6 0.3 convolution_subtract_fusion.1
  315.9 11.7 %cholesky.105 = f32[128,128]{1,0:T(8,128)S(1)} custom-call(f32[128,128]{1,0:T(8,128)S(1)} %convolution_subtract_fusion.1), custom_call_target="Cholesky" | custom-call | tf_op jit(solution)/shard_map/jit(cholesky)/cholesky | solution.py:41
  327.7 0.7 compare_reduce_fusion
  329.8 4.1 %while.1 = (s32[]{:T(128)}, f32[256,256]{1,0:T(8,128)S(1)}, s32[2,2]{1,0:T(2,128)S(1)}, f32[2,128,128]{2,1,0:T(8,128)S(1)}, s32[]{:T(128)}) while((s32[]{:T(128)}, f32[256,256]{1,0:T(8,128)S(1)}, s32[2,2]{1,0:T(2,128)S(1)}, f32[2,128,128]{2,1,0:T(8,128)S(1)}, s32[]{:T(128)}) %tuple.29), condition=%wide.while_cond, body=%wide.while_body.sunk | while | flops 2 | bytes 131189 | solution.py:43
  329.8 0.6 fusion.52
  330.4 1.4 bitcast_dynamic-update-slice_fusion.18
  331.9 0.6 fusion.52
  332.4 1.4 bitcast_dynamic-update-slice_fusion.18
  333.9 19.9 %custom-call.16 = f32[2,128,128]{1,2,0:T(8,128)S(1)} custom-call(f32[2,128,128]{2,1,0:T(8,128)S(1)} %get-tuple-element.9), custom_call_target="InvertDiagBlocksLowerTriangular" | custom-call | tf_op jit(solution)/shard_map/jit(_solve_triangular)/triangular_solve | solution.py:43
  353.8 0.3 fusion.30
  354.0 0.3 convolution_subtract_fusion
  354.3 0.3 fusion.33
  354.6 10.0 %convolution_convert_fusion = bf16[256,4,16,128]{3,0,2,1:T(8,128)(2,1)S(1)} fusion(f32[256,4,16,128]{3,0,2,1:T(8,128)} %fusion.6, f32[128,256]{1,0:T(8,128)S(1)} %fusion.33, f32[128,256]{1,0:T(8,128)S(1)} %fusion.30), kind=kOutput, calls=%fused_computation.30 | convolution fusion | flops 6444613632 | bytes 12845056 | tf_op jit(solution)/shard_map/st,tvxy->svxy/dot_general | solution.py:73
  364.6 4.7 %copy.9 = bf16[256,4,16,128]{3,2,1,0:T(8,128)(2,1)} copy(bf16[256,4,16,128]{3,0,2,1:T(8,128)(2,1)S(1)} %convolution_convert_fusion) | data formatting | bytes 8388608
  369.4 0.4 fusion.26
  369.8 1.1 fusion.28
  (27 shorter events, 0.8 us)
Async XLA Ops:
  34.0 7.7 %copy-start.3 = (f32[4,16,128]{2,1,0:T(8,128)S(1)}, f32[4,16,128]{2,1,0:T(8,128)}, u32[]{:S(2)}) copy-start(f32[4,16,128]{2,1,0:T(8,128)} %param.5) | copy-start | bytes 98308
  34.0 85.1 %all-to-all-start = ((bf16[16,16,4,16,128]{4,3,2,1,0:T(8,128)(2,1)}), bf16[16,16,4,16,128]{4,3,2,1,0:T(8,128)(2,1)}, u32[]{:S(2)}, u32[]{:S(2)}) async-start(bf16[16,16,4,16,128]{4,3,2,1,0:T(8,128)(2,1)} %bitcast_dynamic-update-slice_fusion.1), calls=%async_computation | async-start | bytes 8388608 | tf_op jit(solution)/shard_map/all_to_all | solution.py:49
  41.6 250.1 %all-reduce.5.cloned.1.call-start = ((), (), s32[]{:S(2)}) async-start(), calls=%async_computation.1 | async-start | bytes 1048576 | tf_op jit(solution)/shard_map/psum | solution.py:67
  41.7 87.0 %copy-start.2 = (f32[16,128]{1,0:T(8,128)S(1)}, f32[16,128]{1,0:T(8,128)}, u32[]{:S(2)}) copy-start(f32[16,128]{1,0:T(8,128)} %param.4) | copy-start | bytes 24580
  124.1 8.0 %copy-start = (bf16[16,16,4,16,128]{4,1,0,3,2:T(8,128)(2,1)}, bf16[16,16,4,16,128]{4,1,0,3,2:T(8,128)(2,1)S(1)}, u32[]{:S(2)}) copy-start(bf16[16,16,4,16,128]{4,1,0,3,2:T(8,128)(2,1)S(1)} %copy.5) | copy-start | bytes 12582916
  124.2 17.5 %collective-permute-start = (bf16[256,4,2,128]{3,0,2,1:T(8,128)(2,1)S(1)}, bf16[256,4,2,128]{3,0,2,1:T(8,128)(2,1)S(1)}, u32[]{:S(2)}, u32[]{:S(2)}) collective-permute-start(bf16[256,4,2,128]{3,0,2,1:T(8,128)(2,1)S(1)} %get-tuple-element.24), channel_id=1, source_target_pairs={{0,1},{1,2},{2,3},{3,4},{4,5},{5,6},{6,7},{7,8},{8,9},{9,10},{10,1... | collective-permute-start | bytes 1572872 | tf_op jit(solution)/shard_map/ppermute | solution.py:12
  127.1 14.6 %collective-permute-start.1 = (bf16[256,4,2,128]{3,0,2,1:T(8,128)(2,1)S(1)}, bf16[256,4,2,128]{3,0,2,1:T(8,128)(2,1)S(1)}, u32[]{:S(2)}, u32[]{:S(2)}) collective-permute-start(bf16[256,4,2,128]{3,0,2,1:T(8,128)(2,1)S(1)} %get-tuple-element.25), channel_id=1, source_target_pairs={{1,0},{2,1},{3,2},{4,3},{5,4},{6,5},{7,6},{8,7},{9,8},{10,9},{11,1... | collective-permute-start | bytes 1572872 | tf_op jit(solution)/shard_map/ppermute | solution.py:15
  364.6 4.7 %copy-start.1 = (f32[256,256]{0,1:T(8,128)S(1)}, f32[256,256]{0,1:T(8,128)}, u32[]{:S(2)}) copy-start(f32[256,256]{0,1:T(8,128)} %get-tuple-element.21) | copy-start | bytes 786436
Sparse Core Ops, SparseCore 0:
  184.1 107.5 all-reduce.4
